TPU v7x, 32 devices: a whole 2x2x4 slice. The times are simulated.
32 devices in a mesh: kz: 4 (over x, core), tile: 8 (over z, y).
Axes of the slice: x: 2, y: 2, z: 4, core: 2. Of those that a mesh axis runs over, the one named last changes fastest.
Arguments:
- coil_data: bfloat16 [4, 8, 4, 8, 2, 16, 128], P('kz', 'tile'), may hold values from -6 to 6
- frame_of: int32 [4, 8, 4, 8, 2], P('kz', 'tile'), may hold values from 0 to 999
- basis: bfloat16 [1000, 10], replicated, may hold values from -4 to 4
- sample_pos: float32 [4, 8, 4, 8, 2, 2, 128], P('kz', 'tile'), may hold values from 1.5 to 30.5, as said below
- window_at: int32 [4, 8, 4, 8, 2, 2], P('kz', 'tile'), may hold values from -2 to 639, as said below
- live_count: int32 [4, 8, 4, 8], P('kz', 'tile'), may hold values from 0 to 2, as said below
Outputs:
- image: bfloat16 [4, 640, 102400], P('kz', None, 'tile')
Inputs may be any that keep to these rules, and one draw needn't show every extreme that they name: `live_count`: live slots of a pair are its first ones; destination tiles from 3 up to but not including 8 * 5 // 8 receive every slot from every acquiring device. `window_at`: the first entry (row0) lies in -2 to 78, the second (col0) in 0 to 639. `sample_pos`: the first entry lies in 1.5 to 2.5, the second in 1.5 to 32 - 1.5.
All inputs are finite; a program needn't handle non-finite values.
Results may differ from a plain program's by a relative error of at most 0.0077.
Values may be sent and summed in bfloat16 or wider, within the bound.
No kernel may reach another device: no remote copies, remote signals or barrier semaphores. Data moves between devices by JAX's collectives and lax.ppermute only.
A program may use at most 192 MiB of HBM per device.

v0:
```python
import math
import jax
import jax.numpy as jnp
from jax import lax
from jax.sharding import PartitionSpec as P

PLANE = 640
WIN_ROWS = 4
WIN_COLS = 32


def from_behind(value, axis, steps):
    count = lax.axis_size(axis)
    pairs = [(source, (source + steps) % count) for source in range(count)]
    return lax.ppermute(value, axis, pairs)


def taper(dist):
    inner = 1.0 - (dist / 1.5) ** 2
    return jnp.maximum(inner, 0.0) ** 2


def project(blocks, coeffs):
    count = blocks.shape[0]
    coils = blocks.shape[1] // 2
    ranks = coeffs.shape[1]
    samples = blocks.shape[2]
    data = blocks.astype(jnp.float32).reshape(count, 2, 1, coils, samples)
    scale = coeffs.astype(jnp.float32).reshape(count, 1, ranks, 1, 1)
    return (data * scale).reshape(count, 2 * ranks * coils, samples).astype(jnp.bfloat16)


def grid_tile(proj, offsets, corners, alive, tile_rows, plane):
    count, width, samples = proj.shape
    group = 64
    row_cells = jnp.arange(WIN_ROWS, dtype=jnp.float32)
    col_cells = jnp.arange(WIN_COLS, dtype=jnp.float32)
    cells = jnp.arange(WIN_ROWS * WIN_COLS, dtype=jnp.int32)
    cell_row = cells // WIN_COLS
    cell_col = cells % WIN_COLS

    def step(acc, items):
        values, place, corner, living = items
        row_k = taper(row_cells[None, :, None] - place[:, 0:1, :])
        col_k = taper(col_cells[None, :, None] - place[:, 1:2, :])
        weights = (row_k[:, :, None, :] * col_k[:, None, :, :]).reshape(
            group, WIN_ROWS * WIN_COLS, samples
        )
        weights = (weights * living[:, None, None]).astype(jnp.bfloat16)
        contrib = jnp.einsum("gwb,gcb->gwc", weights, values, preferred_element_type=jnp.float32)
        rows = corner[:, 0:1] + 2 + cell_row[None, :]
        cols = (corner[:, 1:2] + cell_col[None, :]) % plane
        acc = acc.at[rows.reshape(-1), cols.reshape(-1)].add(contrib.reshape(-1, width))
        return (acc, None)

    start = jnp.zeros((tile_rows + 4, plane, width), jnp.float32)
    items = (
        proj.reshape(-1, group, width, samples),
        offsets.reshape(-1, group, 2, samples),
        corners.reshape(-1, group, 2),
        alive.reshape(-1, group),
    )
    acc, _ = lax.scan(step, start, items)
    return acc


def tables(n):
    idx = jnp.arange(n, dtype=jnp.int32)
    phase = (idx[:, None] * idx[None, :] % n).astype(jnp.float32) * (2.0 * math.pi / n)
    return (jnp.cos(phase).astype(jnp.bfloat16), jnp.sin(phase).astype(jnp.bfloat16))


def combine(first, second, half):
    return jnp.concatenate(
        [first[..., :half] - second[..., half:], second[..., :half] + first[..., half:]], axis=-1
    )


def body(coil_data, frame_of, basis, sample_pos, window_at, live_count):
    parts = coil_data.shape[2]
    tiles = coil_data.shape[3]
    slots = coil_data.shape[4]
    pair = coil_data.shape[5]
    samples = coil_data.shape[6]
    width = 2 * basis.shape[1] * (pair // 2)
    half = width // 2
    tile_rows = PLANE // tiles
    raw = lax.all_to_all(
        lax.all_to_all(coil_data, "kz", split_axis=2, concat_axis=0, tiled=True),
        "tile",
        split_axis=3,
        concat_axis=1,
        tiled=True,
    )
    frames = lax.all_to_all(
        lax.all_to_all(frame_of, "kz", split_axis=2, concat_axis=0, tiled=True),
        "tile",
        split_axis=3,
        concat_axis=1,
        tiled=True,
    )
    arrived = project(raw.reshape(-1, pair, samples), basis[frames.reshape(-1)])
    slot_idx = jnp.arange(slots, dtype=jnp.int32)
    counts = live_count.reshape(parts, tiles)
    alive = (slot_idx[None, None, :] < counts[:, :, None]).astype(jnp.float32)
    acc = grid_tile(
        arrived,
        sample_pos.reshape(-1, 2, samples),
        window_at.reshape(-1, 2),
        alive.reshape(-1),
        tile_rows,
        PLANE,
    )
    from_above = from_behind(acc[tile_rows + 2 : tile_rows + 4], "tile", 1)
    from_below = from_behind(acc[0:2], "tile", -1)
    core = acc[2 : tile_rows + 2]
    core = core.at[0:2].add(from_above)
    core = core.at[tile_rows - 2 : tile_rows].add(from_below)
    grid = core.astype(jnp.bfloat16)
    cos_tab, sin_tab = tables(PLANE)
    first = jnp.einsum("xkq,ky->xyq", grid, cos_tab, preferred_element_type=jnp.float32)
    second = jnp.einsum("xkq,ky->xyq", grid, sin_tab, preferred_element_type=jnp.float32)
    mid = combine(first, second, half).astype(jnp.bfloat16)
    columns = lax.all_to_all(mid, "tile", split_axis=1, concat_axis=0, tiled=True)
    first = jnp.einsum("kyq,kx->xyq", columns, cos_tab, preferred_element_type=jnp.float32)
    second = jnp.einsum("kyq,kx->xyq", columns, sin_tab, preferred_element_type=jnp.float32)
    result = (combine(first, second, half) * (1.0 / PLANE)).astype(jnp.bfloat16)
    return result.reshape(1, result.shape[0], -1)


def solution(mesh):
    return jax.shard_map(
        body,
        mesh=mesh,
        in_specs=(
            P("kz", "tile", None, None, None, None, None),
            P("kz", "tile", None, None, None),
            P(),
            P("kz", "tile", None, None, None, None, None),
            P("kz", "tile", None, None, None, None),
            P("kz", "tile", None, None),
        ),
        out_specs=P("kz", None, "tile"),
        check_vma=False,
    )
```

profile of v0, /device:TPU:0, one launch (start us, length us, event | category | flops | bytes accessed | tf_op | source)
XLA Modules:
  0.0 1157.2 jit_solution(10622517823598696329)
XLA Ops:
  0.0 4.4 all-to-all-start.2
  19.8 6.3 all-to-all-start.3
  27.2 5.4 all-to-all-done.3
  37.2 7.0 all-to-all-done.1
  45.9 5.1 fusion.33
  51.0 66.4 %scatter_custom_fusion = f32[53760,160]{1,0:T(8,128)} fusion(s32[8192]{0:T(1024)S(1)} %broadcast_select_fusion, f32[8192,160]{1,0:T(8,128)} %bitcast.76, f32[]{:T(128)} %constant.134.clone.1), kind=kCustom, calls=%fused_computation.4 | custom fusion | flops 1310720 | bytes 34406912
  124.9 4.6 collective-permute-start.1
  129.4 34.4 %slice.123 = f32[51200,160]{1,0:T(8,128)} slice(f32[53760,160]{1,0:T(8,128)} %scatter_custom_fusion), slice={[1280:52480], [0:160]} | slice | bytes 65536000 | tf_op jit(solution)/shard_map/slice | solution.py:116
  164.7 52.2 %copy.108 = f32[80,640,160]{1,0,2:T(8,128)} copy(f32[80,640,160]{2,1,0:T(8,128)} %bitcast.66) | data formatting | bytes 65536000 | tf_op jit(solution)/shard_map/slice | solution.py:116
  222.8 11.5 convert_element_type.79
  234.3 9.7 copy.100
  244.0 30.4 %fusion.13 = f32[640,12800]{0,1} fusion(bf16[640,12800]{0,1:T(8,128)(2,1)} %bitcast.74), kind=kOutput, calls=%fused_computation.31 | convolution fusion | flops 10489856000 | bytes 49152000
  274.5 30.5 %fusion.15 = f32[640,12800]{0,1} fusion(bf16[640,12800]{0,1:T(8,128)(2,1)} %bitcast.75), kind=kOutput, calls=%fused_computation.33 | convolution fusion | flops 10489856000 | bytes 49152000
  305.0 24.4 %fusion.4 = (bf16[80,640,80]{1,2,0:T(8,128)(2,1)S(1)}, bf16[80,640,80]{1,2,0:T(8,128)(2,1)}) fusion(f32[80,640,160]{1,2,0:T(8,128)} %bitcast.71, f32[80,640,160]{1,2,0:T(8,128)} %bitcast.70), kind=kLoop, calls=%fused_computation.11 | loop fusion | flops 16384000 | bytes 81920000 | tf_op jit(solution)/shard_map/convert.2
  329.4 10.3 pad_maximum_fusion
  339.7 38.3 %copy.102 = bf16[80,640,160]{2,0,1:T(8,128)(2,1)} copy(bf16[80,640,160]{1,2,0:T(8,128)(2,1)} %pad_maximum_fusion) | data formatting | bytes 32768000 | tf_op jit(solution)/shard_map/concatenate | solution.py:74
  378.0 571.9 %all_to_all.60 = bf16[80,640,160]{2,0,1:T(8,128)(2,1)} all-to-all(bf16[80,640,160]{2,0,1:T(8,128)(2,1)} %copy.102), channel_id=1, replica_groups=mesh['kz'=4,'tile'=8] {'tile'}, dimensions={1} | all-to-all | bytes 32768000 | tf_op jit(solution)/shard_map/all_to_all | solution.py:124
  950.0 36.0 %copy.103 = bf16[80,8,80,160]{0,1,3,2:T(8,128)(2,1)} copy(bf16[80,8,80,160]{3,0,2,1:T(8,128)(2,1)} %bitcast.67) | data formatting | bytes 32768000 | tf_op jit(solution)/shard_map/all_to_all | solution.py:124
  986.0 37.6 %reshape.322 = bf16[640,12800]{0,1:T(8,128)(2,1)} reshape(bf16[8,80,80,160]{1,0,3,2:T(8,128)(2,1)} %bitcast.68) | data formatting | bytes 32768000
  1023.5 30.4 %fusion.14 = f32[640,12800]{0,1} fusion(bf16[640,12800]{0,1:T(8,128)(2,1)} %reshape.322), kind=kOutput, calls=%fused_computation.32 | convolution fusion | flops 10489856000 | bytes 49152000
  1054.0 30.5 %fusion.16 = f32[640,12800]{0,1} fusion(bf16[640,12800]{0,1:T(8,128)(2,1)} %reshape.322), kind=kOutput, calls=%fused_computation.34 | convolution fusion | flops 10489856000 | bytes 49152000
  1084.5 33.0 %slice_subtract_fusion = (f32[640,80,80]{0,2,1:T(8,128)}, f32[640,80,80]{0,2,1:T(8,128)}) fusion(f32[640,80,160]{0,2,1:T(8,128)} %bitcast.73, f32[640,80,160]{0,2,1:T(8,128)} %bitcast.72), kind=kLoop, calls=%fused_computation.7 | loop fusion | flops 8192000 | bytes 98304000 | tf_op jit(solution)/shard_map/sub | solution.py:75
  1117.5 17.7 %fusion = bf16[640,80,160]{0,2,1:T(8,128)(2,1)} fusion(f32[640,80,80]{0,2,1:T(8,128)} %get-tuple-element.60, f32[640,80,80]{0,2,1:T(8,128)} %get-tuple-element.59), kind=kLoop, calls=%fused_computation.3 | loop fusion | flops 24576000 | bytes 49152000 | tf_op jit(solution)/shard_map/convert_element_type | solution.py:127
  1135.2 21.9 %copy.104 = bf16[1,640,12800]{2,1,0:T(8,128)(2,1)} copy(bf16[1,640,12800]{1,2,0:T(8,128)(2,1)} %bitcast.69) | data formatting | bytes 32768000 | tf_op jit(solution)/shard_map/convert_element_type | solution.py:127
  (51 shorter events, 36.7 us)
Async XLA Ops:
  0.0 16.4 %copy-start.2 = (s32[2]{0:T(128)S(1)}, s32[2]{0:T(128)}, u32[]{:S(2)}) copy-start(s32[2]{0:T(128)} %constant.155) | copy-start | bytes 28
  0.0 26.1 %copy-start.1 = (s32[2]{0:T(128)S(1)}, s32[2]{0:T(128)}, u32[]{:S(2)}) copy-start(s32[2]{0:T(128)} %constant.152) | copy-start | bytes 28
  0.0 26.2 %copy-start = (bf16[1000,10]{0,1:T(8,128)(2,1)S(1)}, bf16[1000,10]{0,1:T(8,128)(2,1)}, u32[]{:S(2)}) copy-start(bf16[1000,10]{0,1:T(8,128)(2,1)} %param.12) | copy-start | bytes 60004
  0.0 10.3 all-to-all-start.2
  10.4 9.4 all-to-all-start
  19.8 12.9 %all-to-all-start.3 = ((s32[4,1,1,8,2]{0,4,2,1,3:T(2,128)}), s32[4,1,1,8,2]{0,4,2,1,3:T(2,128)S(1)}, u32[]{:S(2)}, u32[]{:S(2)}) async-start(s32[4,1,1,8,2]{0,4,2,1,3:T(2,128)} %copy.89), calls=%async_computation.3 | async-start | bytes 16384 | tf_op jit(solution)/shard_map/all_to_all | solution.py:95
  32.6 11.6 %all-to-all-start.1 = ((bf16[4,1,1,8,2,16,128]{6,5,4,0,2,1,3:T(8,128)(2,1)}), bf16[4,1,1,8,2,16,128]{6,5,4,0,2,1,3:T(8,128)(2,1)S(1)}, u32[]{:S(2)}, u32[]{:S(2)}) async-start(bf16[4,1,1,8,2,16,128]{6,5,4,0,2,1,3:T(8,128)(2,1)} %copy.85), calls=%async_computation.1 | async-start | bytes 524288 | tf_op jit(solution)/shard_map/all_to_all | solution.py:88
  123.4 93.5 %collective-permute-start = (f32[2,640,160]{1,0,2:T(2,128)}, f32[2,640,160]{1,0,2:T(2,128)}, u32[]{:S(2)}, u32[]{:S(2)}) collective-permute-start(f32[2,640,160]{1,0,2:T(2,128)} %copy.110), channel_id=1, source_target_pairs={{0,1},{1,2},{2,3},{3,4},{4,5},{5,6},{6,7},{7,0},{8,9},{9,10},{10,1... | collective-permute-start | bytes 2457608 | tf_op jit(solution)/shard_map/ppermute | solution.py:15
  124.9 94.6 %collective-permute-start.1 = (f32[2,640,160]{1,0,2:T(2,128)}, f32[2,640,160]{1,0,2:T(2,128)S(1)}, u32[]{:S(2)}, u32[]{:S(2)}) collective-permute-start(f32[2,640,160]{1,0,2:T(2,128)} %copy.111), channel_id=1, source_target_pairs={{0,7},{1,0},{2,1},{3,2},{4,3},{5,4},{6,5},{7,6},{8,15},{9,8},{10,9... | collective-permute-start | bytes 2457608 | tf_op jit(solution)/shard_map/ppermute | solution.py:15
where the time goes:
time: 1170 us; the launch traced here: 1160 us
  blocking collectives  572 us (49%)
  local copies, waits for them, and re-layouts  243 us (21%)
  other arithmetic  178 us (15%)
  matrix products  127 us (11%)
  starting transfers between devices  22.3 us (2%)
  waiting for transfers between devices  15 us (1%)
    all_to_all x1, blocking collectives, body(): lax.all_to_all(mid, 'tile', split_axis=1, concat_axis=0, tiled=True)  572 us
    unnamed x4, matrix products  122 us
    slice x2, local copies, waits for them, and re-layouts, body(): core = acc[2:tile_rows + 2]  86.6 us
    unnamed x4, other arithmetic  66.7 us
    unnamed x9, local copies, waits for them, and re-layouts  38.6 us
    concatenate x1, local copies, waits for them, and re-layouts, combine(): jnp.concatenate([first[..., :half] - second[..., half:], second[..., :hal...  38.3 us
    all_to_all x1, local copies, waits for them, and re-layouts, body(): lax.all_to_all(mid, 'tile', split_axis=1, concat_axis=0, tiled=True)  36 us
    sub x1, other arithmetic, combine(): first[..., :half] - second[..., half:]  33 us
  transfers between devices with their start and end apart: 6, of which 3 were waited for; matrix products, arithmetic and copies ran while one was open for 9% of the time, Pallas kernels for 0%

commit v1 on v0

--- a/solution.py
+++ b/solution.py
@@ -121,7 +121,10 @@
     first = jnp.einsum("xkq,ky->xyq", grid, cos_tab, preferred_element_type=jnp.float32)
     second = jnp.einsum("xkq,ky->xyq", grid, sin_tab, preferred_element_type=jnp.float32)
     mid = combine(first, second, half).astype(jnp.bfloat16)
-    columns = lax.all_to_all(mid, "tile", split_axis=1, concat_axis=0, tiled=True)
+    columns = jnp.concatenate(
+        lax.all_to_all(jnp.stack(jnp.split(mid, lax.axis_size("tile"), axis=1)), "tile", 0, 0),
+        axis=0,
+    )
     first = jnp.einsum("kyq,kx->xyq", columns, cos_tab, preferred_element_type=jnp.float32)
     second = jnp.einsum("kyq,kx->xyq", columns, sin_tab, preferred_element_type=jnp.float32)
     result = (combine(first, second, half) * (1.0 / PLANE)).astype(jnp.bfloat16)

time: 1170 us -> 1110 us (0.949)
  local copies, waits for them, and re-layouts: 243 us -> 168 us
  other arithmetic: 178 us -> 190 us
    concatenate x1 -> x0, local copies, waits for them, and re-layouts: 38.3 us -> none  [combine(): jnp.concatenate([first[..., :half] - second[..., half:], second[..., :hal...]
    all_to_all x1 -> x0, local copies, waits for them, and re-layouts: 36 us -> none  [body(): lax.all_to_all(mid, 'tile', split_axis=1, concat_axis=0, tiled=True)]
    unnamed x9 -> x10, local copies, waits for them, and re-layouts: 38.6 us -> 2.86 us
    reshape x0 -> x1, local copies, waits for them, and re-layouts: none -> 35.2 us  [body(): jnp.concatenate(lax.all_to_all(jnp.stack(jnp.split(mid, lax.axis_size('ti...]
    unnamed x4 -> x11, other arithmetic: 66.7 us -> 86.4 us
    another operation x1 -> x2, other arithmetic: 24.4 us -> 27.1 us
where the time goes in v1:
time: 1110 us; the launch traced here: 1100 us
  blocking collectives  572 us (52%)
  other arithmetic  190 us (17%)
  local copies, waits for them, and re-layouts  168 us (15%)
  matrix products  135 us (12%)
  starting transfers between devices  22.3 us (2%)
  waiting for transfers between devices  15 us (1%)
    all_to_all x1, blocking collectives, body(): lax.all_to_all(jnp.stack(jnp.split(mid, lax.axis_size('tile'), axis=1)),...  572 us
    unnamed x4, matrix products  130 us
    slice x2, local copies, waits for them, and re-layouts, body(): core = acc[2:tile_rows + 2]  86.6 us
    unnamed x11, other arithmetic  86.4 us
    reshape x1, local copies, waits for them, and re-layouts, body(): jnp.concatenate(lax.all_to_all(jnp.stack(jnp.split(mid, lax.axis_size('ti...  35.2 us
    sub x1, other arithmetic, combine(): first[..., :half] - second[..., half:]  33 us
    another operation x1, other arithmetic  24.4 us
  transfers between devices with their start and end apart: 6, of which 3 were waited for; matrix products, arithmetic and copies ran while one was open for 9% of the time, Pallas kernels for 0%

profile of v1, /device:TPU:0, one launch (start us, length us, event | category | flops | bytes accessed | tf_op | source)
XLA Modules:
  0.0 1102.2 jit_solution(10829402923318572074)
XLA Ops:
  0.0 4.4 all-to-all-start.2
  10.4 3.4 all-to-all-start
  19.8 6.3 all-to-all-start.3
  27.2 5.4 all-to-all-done.3
  32.6 3.4 all-to-all-start.1
  37.2 7.0 all-to-all-done.1
  45.9 5.1 fusion.56
  51.1 66.5 %scatter_custom_fusion = f32[53760,160]{1,0:T(8,128)} fusion(s32[8192]{0:T(1024)S(1)} %broadcast_select_fusion, f32[8192,160]{1,0:T(8,128)} %bitcast.106, f32[]{:T(128)} %constant.134.clone.1), kind=kCustom, calls=%fused_computation.18 | custom fusion | flops 1310720 | bytes 34406912
  117.5 3.5 fusion.54
  124.9 4.6 collective-permute-start.1
  129.5 34.4 %slice.123 = f32[51200,160]{1,0:T(8,128)} slice(f32[53760,160]{1,0:T(8,128)} %scatter_custom_fusion), slice={[1280:52480], [0:160]} | slice | bytes 65536000 | tf_op jit(solution)/shard_map/slice | solution.py:116
  164.7 52.2 %copy.111 = f32[80,640,160]{1,0,2:T(8,128)} copy(f32[80,640,160]{2,1,0:T(8,128)} %bitcast.95) | data formatting | bytes 65536000 | tf_op jit(solution)/shard_map/slice | solution.py:116
  222.9 11.5 %convert_element_type.79 = bf16[80,640,160]{1,0,2:T(8,128)(2,1)S(1)} convert(f32[80,640,160]{1,0,2:T(8,128)} %fusion.35) | non-fusion elementwise | flops 8192000 | bytes 49152000 | tf_op jit(solution)/shard_map/convert_element_type | solution.py:119
  234.5 9.7 copy.103
  244.2 30.3 %fusion.36 = f32[640,12800]{0,1} fusion(bf16[640,12800]{0,1:T(8,128)(2,1)} %bitcast.102), kind=kOutput, calls=%fused_computation.68 | convolution fusion | flops 10489856000 | bytes 49152000
  274.5 38.4 %fusion.38 = f32[640,12800]{0,1} fusion(bf16[640,12800]{0,1:T(8,128)(2,1)} %bitcast.103), kind=kOutput, calls=%fused_computation.70 | convolution fusion | flops 10489856000 | bytes 49152000
  312.9 24.4 %fusion.3 = (bf16[80,640,80]{1,2,0:T(8,128)(2,1)S(1)}, bf16[80,640,80]{1,2,0:T(8,128)(2,1)}) fusion(f32[80,640,160]{1,2,0:T(8,128)} %bitcast.98, f32[80,640,160]{1,2,0:T(8,128)} %bitcast.99), kind=kLoop, calls=%fused_computation.23 | loop fusion | flops 16384000 | bytes 81920000 | tf_op jit(solution)/shard_map/convert.3
  361.4 571.5 %all_to_all.47 = bf16[8,80,80,160]{2,3,1,0:T(8,128)(2,1)} all-to-all(bf16[8,80,80,160]{2,3,1,0:T(8,128)(2,1)} %fusion.29), channel_id=1, replica_groups=mesh['kz'=4,'tile'=8] {'tile'}, dimensions={0} | all-to-all | bytes 32768000 | tf_op jit(solution)/shard_map/all_to_all | solution.py:125
  933.0 35.2 %copy.105 = bf16[640,80,160]{0,2,1:T(8,128)(2,1)} copy(bf16[640,80,160]{1,2,0:T(8,128)(2,1)} %bitcast.96) | data formatting | bytes 32768000 | tf_op jit(solution)/shard_map/reshape | solution.py:124
  968.2 30.3 %fusion.37 = f32[640,12800]{0,1} fusion(bf16[640,12800]{0,1:T(8,128)(2,1)} %bitcast.104), kind=kOutput, calls=%fused_computation.69 | convolution fusion | flops 10489856000 | bytes 49152000
  998.5 30.6 %fusion.39 = f32[640,12800]{0,1} fusion(bf16[640,12800]{0,1:T(8,128)(2,1)} %bitcast.105), kind=kOutput, calls=%fused_computation.71 | convolution fusion | flops 10489856000 | bytes 49152000
  1029.1 33.0 %slice_subtract_fusion = (f32[640,80,80]{0,2,1:T(8,128)}, f32[640,80,80]{0,2,1:T(8,128)}) fusion(f32[640,80,160]{0,2,1:T(8,128)} %bitcast.101, f32[640,80,160]{0,2,1:T(8,128)} %bitcast.100), kind=kLoop, calls=%fused_computation.21 | loop fusion | flops 8192000 | bytes 98304000 | tf_op jit(solution)/shard_map/sub | solution.py:75
  1062.2 17.7 %fusion = bf16[640,80,160]{0,2,1:T(8,128)(2,1)} fusion(f32[640,80,80]{0,2,1:T(8,128)} %get-tuple-element.60, f32[640,80,80]{0,2,1:T(8,128)} %get-tuple-element.59), kind=kLoop, calls=%fused_computation.3 | loop fusion | flops 24576000 | bytes 49152000 | tf_op jit(solution)/shard_map/convert_element_type | solution.py:130
  1079.9 21.9 %copy.107 = bf16[1,640,12800]{2,1,0:T(8,128)(2,1)} copy(bf16[1,640,12800]{1,2,0:T(8,128)(2,1)} %bitcast.97) | data formatting | bytes 32768000 | tf_op jit(solution)/shard_map/convert_element_type | solution.py:130
  (58 shorter events, 50.6 us)
Async XLA Ops:
  0.0 16.4 %copy-start.3 = (s32[2]{0:T(128)S(1)}, s32[2]{0:T(128)}, u32[]{:S(2)}) copy-start(s32[2]{0:T(128)} %constant.155) | copy-start | bytes 28
  0.0 26.1 %copy-start.2 = (s32[2]{0:T(128)S(1)}, s32[2]{0:T(128)}, u32[]{:S(2)}) copy-start(s32[2]{0:T(128)} %constant.152) | copy-start | bytes 28
  0.0 26.2 %copy-start.1 = (bf16[1000,10]{0,1:T(8,128)(2,1)S(1)}, bf16[1000,10]{0,1:T(8,128)(2,1)}, u32[]{:S(2)}) copy-start(bf16[1000,10]{0,1:T(8,128)(2,1)} %param.12) | copy-start | bytes 60004
  0.0 10.3 all-to-all-start.2
  10.4 9.4 all-to-all-start
  19.8 12.9 %all-to-all-start.3 = ((s32[4,1,1,8,2]{0,4,2,1,3:T(2,128)}), s32[4,1,1,8,2]{0,4,2,1,3:T(2,128)S(1)}, u32[]{:S(2)}, u32[]{:S(2)}) async-start(s32[4,1,1,8,2]{0,4,2,1,3:T(2,128)} %copy.92), calls=%async_computation.3 | async-start | bytes 16384 | tf_op jit(solution)/shard_map/all_to_all | solution.py:95
  32.6 11.6 %all-to-all-start.1 = ((bf16[4,1,1,8,2,16,128]{6,5,4,0,2,1,3:T(8,128)(2,1)}), bf16[4,1,1,8,2,16,128]{6,5,4,0,2,1,3:T(8,128)(2,1)S(1)}, u32[]{:S(2)}, u32[]{:S(2)}) async-start(bf16[4,1,1,8,2,16,128]{6,5,4,0,2,1,3:T(8,128)(2,1)} %copy.88), calls=%async_computation.1 | async-start | bytes 524288 | tf_op jit(solution)/shard_map/all_to_all | solution.py:88
  123.4 93.5 %collective-permute-start = (f32[2,640,160]{1,0,2:T(2,128)}, f32[2,640,160]{1,0,2:T(2,128)}, u32[]{:S(2)}, u32[]{:S(2)}) collective-permute-start(f32[2,640,160]{1,0,2:T(2,128)} %copy.113), channel_id=1, source_target_pairs={{0,1},{1,2},{2,3},{3,4},{4,5},{5,6},{6,7},{7,0},{8,9},{9,10},{10,1... | collective-permute-start | bytes 2457608 | tf_op jit(solution)/shard_map/ppermute | solution.py:15
  124.9 94.6 %collective-permute-start.1 = (f32[2,640,160]{1,0,2:T(2,128)}, f32[2,640,160]{1,0,2:T(2,128)S(1)}, u32[]{:S(2)}, u32[]{:S(2)}) collective-permute-start(f32[2,640,160]{1,0,2:T(2,128)} %copy.114), channel_id=1, source_target_pairs={{0,7},{1,0},{2,1},{3,2},{4,3},{5,4},{6,5},{7,6},{8,15},{9,8},{10,9... | collective-permute-start | bytes 2457608 | tf_op jit(solution)/shard_map/ppermute | solution.py:15
  337.3 5.0 copy-start
